TPU v7x, 128 devices: a whole 4x4x4 slice. The times are simulated.
128 devices in a mesh: mode: 8 (over z, y_hi), slab: 16 (over x, y_lo, core).
Axes of the slice: x: 4, y: 4 (y_hi: 2, y_lo: 2; y = y_hi * 2 + y_lo), z: 4, core: 2. Of those that a mesh axis runs over, the one named last changes fastest.
Arguments:
- modes: bfloat16 [48, 3, 32, 256, 128], P('mode', None, 'slab'), may hold values from -100 to 100
- volume: float32 [32, 256, 128], P(None, ('mode', 'slab')), may hold values from 0.5 to 24
Outputs:
- convective: float32 [2304, 48], P(('mode', 'slab'))
- dissipation: float32 [48, 48], replicated
All inputs are finite; a program needn't handle non-finite values.
Results may differ from a plain program's by a relative error of at most 0.0043.
Values may be sent and summed in bfloat16 or wider, within the bound.
A program may use at most 128 MiB of HBM per device.

v0:
```python
import math
import jax
import jax.numpy as jnp
from jax import lax
from jax.sharding import PartitionSpec as P

viscosity = 0.05


def extended(block, sides, width):
    for axis, dim in sides:
        count = lax.axis_size(axis)
        forward = [(i, i + 1) for i in range(count - 1)]
        backward = [(target, source) for source, target in forward]
        low = lax.ppermute(
            lax.slice_in_dim(block, block.shape[dim] - width, None, axis=dim), axis, forward
        )
        high = lax.ppermute(lax.slice_in_dim(block, 0, width, axis=dim), axis, backward)
        block = jnp.concatenate([low, block, high], axis=dim)
    return block


def stencil(padded, dim, length):
    shifted = [
        lax.slice_in_dim(padded, offset, offset + length, axis=dim).astype(jnp.float32)
        for offset in range(5)
    ]
    return (shifted[0] - 8.0 * shifted[1] + 8.0 * shifted[3] - shifted[4]) / 12.0


def gradient_fields(centre, x_padded, y_padded):
    z_padded = jnp.concatenate([centre[..., -2:], centre, centre[..., :2]], axis=4)
    along_x = stencil(x_padded, 2, centre.shape[2])
    along_y = stencil(y_padded, 3, centre.shape[3])
    along_z = stencil(z_padded, 4, centre.shape[4])
    return jnp.stack([along_x, along_y, along_z], axis=2).astype(jnp.bfloat16)


def regroup(stacked):
    return lax.all_to_all(
        lax.all_to_all(stacked, "mode", split_axis=3, concat_axis=0, tiled=True),
        "slab",
        split_axis=3,
        concat_axis=2,
        tiled=True,
    )


def contract(values, grad_all, weights, limit):
    mode_count = values.shape[0]
    cell_count = weights.size
    block_size = math.gcd(cell_count, limit)
    flat_values = values.reshape(mode_count, 3, cell_count)
    flat_grads = grad_all.reshape(mode_count, 3, 3, cell_count)
    flat_weights = weights.reshape(cell_count)

    def one_step(number, running):
        first_cell = number * block_size
        piece_values = lax.dynamic_slice_in_dim(flat_values, first_cell, block_size, 2)
        piece_grads = lax.dynamic_slice_in_dim(flat_grads, first_cell, block_size, 3)
        piece_weights = lax.dynamic_slice_in_dim(flat_weights, first_cell, block_size, 0)
        values_wide = piece_values.astype(jnp.float32)
        grads_wide = piece_grads.astype(jnp.float32)
        carried = values_wide[:, None, None, 0, :] * grads_wide[None, :, :, 0, :]
        carried = carried + values_wide[:, None, None, 1, :] * grads_wide[None, :, :, 1, :]
        carried = carried + values_wide[:, None, None, 2, :] * grads_wide[None, :, :, 2, :]
        carried = (
            (carried * piece_weights)
            .astype(jnp.bfloat16)
            .reshape(mode_count * mode_count, 3 * block_size)
        )
        conv_add = lax.dot_general(
            piece_values.reshape(mode_count, 3 * block_size),
            carried,
            (((1,), (1,)), ((), ())),
            preferred_element_type=jnp.float32,
        )
        weighted = (
            (grads_wide * piece_weights).astype(jnp.bfloat16).reshape(mode_count, 9 * block_size)
        )
        diss_add = lax.dot_general(
            piece_grads.reshape(mode_count, 9 * block_size),
            weighted,
            (((1,), (1,)), ((), ())),
            preferred_element_type=jnp.float32,
        )
        return (running[0] + conv_add, running[1] + diss_add)

    start_conv = jnp.zeros((mode_count, mode_count * mode_count), jnp.float32)
    start_diss = jnp.zeros((mode_count, mode_count), jnp.float32)
    conv_sum, diss_sum = lax.fori_loop(
        0, cell_count // block_size, one_step, (start_conv, start_diss)
    )
    return (conv_sum.reshape(mode_count * mode_count, mode_count), diss_sum)


def per_device(modes, volume):
    x_padded = extended(modes, (("slab", 2),), 2)
    y_padded = jnp.pad(modes, ((0, 0), (0, 0), (0, 0), (2, 2), (0, 0)))
    local_grads = gradient_fields(modes, x_padded, y_padded)
    local_count = modes.shape[0]
    stacked = jnp.concatenate(
        [modes, local_grads.reshape((local_count, 9) + modes.shape[2:])], axis=1
    )
    regrouped = regroup(stacked)
    values = regrouped[:, :3]
    grad_all = regrouped[:, 3:].reshape((regrouped.shape[0], 3, 3) + regrouped.shape[2:])
    conv_part, diss_part = contract(values, grad_all, volume, 1024)
    conv_sum = lax.psum_scatter(conv_part, ("mode", "slab"), scatter_dimension=0, tiled=True)
    diss_sum = lax.psum(diss_part, ("mode", "slab"))
    cell_total = (
        volume.shape[0]
        * volume.shape[1]
        * volume.shape[2]
        * lax.axis_size("mode")
        * lax.axis_size("slab")
    )
    convective = conv_sum * (1.0 / math.sqrt(cell_total))
    dissipation = diss_sum * (viscosity / cell_total)
    return (convective, dissipation)


def solution(mesh):
    placed = (P("mode", None, "slab", None, None), P(None, ("mode", "slab"), None))
    return jax.shard_map(
        per_device,
        mesh=mesh,
        in_specs=placed,
        out_specs=(P(("mode", "slab"), None), P()),
        check_vma=False,
    )
```

profile of v0, /device:TPU:1, one launch (start us, length us, event | category | flops | bytes accessed | tf_op | source)
XLA Modules:
  0.0 1076.9 jit_solution(17785046774700136053)
XLA Ops:
  17.1 21.5 %collective-permute-done.1 = bf16[6,3,2,256,128]{4,3,2,1,0:T(8,128)(2,1)S(1)} collective-permute-done((bf16[6,3,2,256,128]{4,3,2,1,0:T(8,128)(2,1)}, bf16[6,3,2,256,128]{4,3,2,1,0:T(8,128)(2,1)S(1)}, u32[]{:S(2)}, u32[]{:S(2)}) %collective-permute-start.1) | collective-permute-done | bytes 2359328 | tf_op jit(solution)/shard_map/ppermute | solution.py:18
  38.6 25.6 %collective-permute-done = bf16[6,3,2,256,128]{4,3,2,1,0:T(8,128)(2,1)S(1)} collective-permute-done((bf16[6,3,2,256,128]{4,3,2,1,0:T(8,128)(2,1)}, bf16[6,3,2,256,128]{4,3,2,1,0:T(8,128)(2,1)S(1)}, u32[]{:S(2)}, u32[]{:S(2)}) %collective-permute-start) | collective-permute-done | bytes 2359328 | tf_op jit(solution)/shard_map/ppermute | solution.py:15
  85.1 17.6 %copy.54 = bf16[6,12,2,256,128]{4,2,1,0,3:T(2,128)(2,1)S(1)} copy(bf16[6,12,2,256,128]{4,3,2,1,0:T(8,128)(2,1)} %pad_maximum_fusion) | data formatting | bytes 18874368 | tf_op jit(solution)/shard_map/concatenate | solution.py:102
  102.7 69.1 %all_to_all.36 = bf16[6,12,2,256,128]{4,2,1,0,3:T(2,128)(2,1)} all-to-all(bf16[6,12,2,256,128]{4,2,1,0,3:T(2,128)(2,1)S(1)} %copy.54), channel_id=1, replica_groups=mesh['mode'=8,'slab'=16] {'mode'}, dimensions={3} | all-to-all | bytes 18874368 | tf_op jit(solution)/shard_map/all_to_all | solution.py:41
  181.6 10.4 copy.56
  192.1 14.8 %copy.57 = bf16[48,12,2,32,128]{4,2,1,0,3:T(2,128)(2,1)} copy(bf16[48,12,2,32,128]{4,3,2,1,0:T(8,128)(2,1)} %bitcast.74) | data formatting | bytes 18874368 | tf_op jit(solution)/shard_map/all_to_all | solution.py:41
  206.9 29.7 %all-to-all-start.1 = ((bf16[48,12,2,32,128]{4,2,1,0,3:T(2,128)(2,1)}), bf16[48,12,2,32,128]{4,2,1,0,3:T(2,128)(2,1)}, u32[]{:S(2)}, u32[]{:S(2)}) async-start(bf16[48,12,2,32,128]{4,2,1,0,3:T(2,128)(2,1)} %copy.57), calls=%async_computation.1 | async-start | bytes 18874368 | tf_op jit(solution)/shard_map/all_to_all | solution.py:40
  236.8 143.3 %all-to-all-done.1 = bf16[48,12,2,32,128]{4,2,1,0,3:T(2,128)(2,1)} async-done(((bf16[48,12,2,32,128]{4,2,1,0,3:T(2,128)(2,1)}), bf16[48,12,2,32,128]{4,2,1,0,3:T(2,128)(2,1)}, u32[]{:S(2)}, u32[]{:S(2)}) %all-to-all-start.1) | async-done | bytes 9437216 | tf_op jit(solution)/shard_map/all_to_all | solution.py:40
  389.5 10.3 copy.59
  415.6 16.2 %reshape_reshape.3 = bf16[48,3,3,8192]{3,0,2,1:T(8,128)(2,1)} reshape(bf16[48,9,32,2,128]{4,3,2,0,1:T(2,128)(2,1)} %copy.61) | data formatting | bytes 14155776 | tf_op jit(solution)/shard_map/reshape;reshape | solution.py:54
  442.0 407.7 %while.16 = (s32[]{:T(128)}, f32[48,2304]{1,0:T(8,128)}, f32[48,48]{1,0:T(8,128)S(1)}, bf16[48,3,8192]{2,1,0:T(4,128)(2,1)}, bf16[48,3,3,8192]{3,0,2,1:T(8,128)(...) while((s32[]{:T(128)}, f32[48,2304]{1,0:T(8,128)}, ...), condition=%wide.region_1.2_spmd.clone, body=%wide.region_0.1_spmd.clone.sunk | while | flops 773485056 | bytes 75239088 | solution.py:91
  452.5 19.9 %multiply_convert_fusion.9 = bf16[48,48,3,1024]{3,2,1,0:T(4,128)(2,1)S(1)} fusion(f32[1024]{0:T(1024)S(1)} %dynamic_slice.40, f32[48,3,1024]{2,1,0:T(4,128)} %copy.84, f32[48,1024]{1,0:T(8,128)} %get-tuple-element.238, f32[48,3,1024]{2,1,0:T(4,128)} %copy.85, f32[48,1024]{1,0:T(8,128)} %get-tuple-element.240, f32[48,3,1024]{2,1,0:T(4,128)} %copy.86, ...), kind=kLoop, calls=%fused_computation.clone.1 | loop fusion | flops 49545216 | bytes 16519168 | tf_op jit(solution)/shard_map/while/body/eval_jaxpr/convert_element_type | solution.py:69
  472.4 10.4 copy.88
  503.5 19.9 %multiply_convert_fusion.9 = bf16[48,48,3,1024]{3,2,1,0:T(4,128)(2,1)S(1)} fusion(f32[1024]{0:T(1024)S(1)} %dynamic_slice.40, f32[48,3,1024]{2,1,0:T(4,128)} %copy.84, f32[48,1024]{1,0:T(8,128)} %get-tuple-element.238, f32[48,3,1024]{2,1,0:T(4,128)} %copy.85, f32[48,1024]{1,0:T(8,128)} %get-tuple-element.240, f32[48,3,1024]{2,1,0:T(4,128)} %copy.86, ...), kind=kLoop, calls=%fused_computation.clone.1 | loop fusion | flops 49545216 | bytes 16519168 | tf_op jit(solution)/shard_map/while/body/eval_jaxpr/convert_element_type | solution.py:69
  523.4 10.4 copy.88
  554.4 19.9 %multiply_convert_fusion.9 = bf16[48,48,3,1024]{3,2,1,0:T(4,128)(2,1)S(1)} fusion(f32[1024]{0:T(1024)S(1)} %dynamic_slice.40, f32[48,3,1024]{2,1,0:T(4,128)} %copy.84, f32[48,1024]{1,0:T(8,128)} %get-tuple-element.238, f32[48,3,1024]{2,1,0:T(4,128)} %copy.85, f32[48,1024]{1,0:T(8,128)} %get-tuple-element.240, f32[48,3,1024]{2,1,0:T(4,128)} %copy.86, ...), kind=kLoop, calls=%fused_computation.clone.1 | loop fusion | flops 49545216 | bytes 16519168 | tf_op jit(solution)/shard_map/while/body/eval_jaxpr/convert_element_type | solution.py:69
  574.3 10.4 copy.88
  584.7 10.1 convolution_add_fusion.2
  605.4 19.9 %multiply_convert_fusion.9 = bf16[48,48,3,1024]{3,2,1,0:T(4,128)(2,1)S(1)} fusion(f32[1024]{0:T(1024)S(1)} %dynamic_slice.40, f32[48,3,1024]{2,1,0:T(4,128)} %copy.84, f32[48,1024]{1,0:T(8,128)} %get-tuple-element.238, f32[48,3,1024]{2,1,0:T(4,128)} %copy.85, f32[48,1024]{1,0:T(8,128)} %get-tuple-element.240, f32[48,3,1024]{2,1,0:T(4,128)} %copy.86, ...), kind=kLoop, calls=%fused_computation.clone.1 | loop fusion | flops 49545216 | bytes 16519168 | tf_op jit(solution)/shard_map/while/body/eval_jaxpr/convert_element_type | solution.py:69
  625.3 10.4 copy.88
  635.6 10.1 convolution_add_fusion.2
  656.4 19.9 %multiply_convert_fusion.9 = bf16[48,48,3,1024]{3,2,1,0:T(4,128)(2,1)S(1)} fusion(f32[1024]{0:T(1024)S(1)} %dynamic_slice.40, f32[48,3,1024]{2,1,0:T(4,128)} %copy.84, f32[48,1024]{1,0:T(8,128)} %get-tuple-element.238, f32[48,3,1024]{2,1,0:T(4,128)} %copy.85, f32[48,1024]{1,0:T(8,128)} %get-tuple-element.240, f32[48,3,1024]{2,1,0:T(4,128)} %copy.86, ...), kind=kLoop, calls=%fused_computation.clone.1 | loop fusion | flops 49545216 | bytes 16519168 | tf_op jit(solution)/shard_map/while/body/eval_jaxpr/convert_element_type | solution.py:69
  676.3 10.4 copy.88
  707.4 19.9 %multiply_convert_fusion.9 = bf16[48,48,3,1024]{3,2,1,0:T(4,128)(2,1)S(1)} fusion(f32[1024]{0:T(1024)S(1)} %dynamic_slice.40, f32[48,3,1024]{2,1,0:T(4,128)} %copy.84, f32[48,1024]{1,0:T(8,128)} %get-tuple-element.238, f32[48,3,1024]{2,1,0:T(4,128)} %copy.85, f32[48,1024]{1,0:T(8,128)} %get-tuple-element.240, f32[48,3,1024]{2,1,0:T(4,128)} %copy.86, ...), kind=kLoop, calls=%fused_computation.clone.1 | loop fusion | flops 49545216 | bytes 16519168 | tf_op jit(solution)/shard_map/while/body/eval_jaxpr/convert_element_type | solution.py:69
  727.3 10.4 copy.88
  758.3 19.9 %multiply_convert_fusion.9 = bf16[48,48,3,1024]{3,2,1,0:T(4,128)(2,1)S(1)} fusion(f32[1024]{0:T(1024)S(1)} %dynamic_slice.40, f32[48,3,1024]{2,1,0:T(4,128)} %copy.84, f32[48,1024]{1,0:T(8,128)} %get-tuple-element.238, f32[48,3,1024]{2,1,0:T(4,128)} %copy.85, f32[48,1024]{1,0:T(8,128)} %get-tuple-element.240, f32[48,3,1024]{2,1,0:T(4,128)} %copy.86, ...), kind=kLoop, calls=%fused_computation.clone.1 | loop fusion | flops 49545216 | bytes 16519168 | tf_op jit(solution)/shard_map/while/body/eval_jaxpr/convert_element_type | solution.py:69
  778.2 10.4 copy.88
  788.6 10.1 convolution_add_fusion.2
  809.3 19.9 %multiply_convert_fusion.9 = bf16[48,48,3,1024]{3,2,1,0:T(4,128)(2,1)S(1)} fusion(f32[1024]{0:T(1024)S(1)} %dynamic_slice.40, f32[48,3,1024]{2,1,0:T(4,128)} %copy.84, f32[48,1024]{1,0:T(8,128)} %get-tuple-element.238, f32[48,3,1024]{2,1,0:T(4,128)} %copy.85, f32[48,1024]{1,0:T(8,128)} %get-tuple-element.240, f32[48,3,1024]{2,1,0:T(4,128)} %copy.86, ...), kind=kLoop, calls=%fused_computation.clone.1 | loop fusion | flops 49545216 | bytes 16519168 | tf_op jit(solution)/shard_map/while/body/eval_jaxpr/convert_element_type | solution.py:69
  829.2 10.4 copy.88
  849.7 70.5 %psum.7 = f32[48,48]{1,0:T(8,128)S(1)} all-reduce(f32[48,48]{1,0:T(8,128)S(1)} %get-tuple-element.113), channel_id=1, replica_groups=mesh['mode'=8,'slab'=16] {'mode','slab'}, use_global_device_ids=true, to_apply=%region_3.4 | all-reduce | flops 2304 | bytes 18432 | tf_op jit(solution)/shard_map/psum | solution.py:110
  923.7 145.1 %all-reduce.4.cloned.1.call-done = f32[2304,48]{1,0:T(8,128)} async-done(((f32[2304,48]{1,0:T(8,128)}), f32[2304,48]{1,0:T(8,128)}) %all-reduce.4.cloned.1.call-update) | async-done | bytes 442384
  (123 shorter events, 215.9 us)
Async XLA Ops:
  7.2 57.0 %copy-start = (bf16[6,3,2,256,128]{4,3,2,1,0:T(8,128)(2,1)S(1)}, bf16[6,3,2,256,128]{4,3,2,1,0:T(8,128)(2,1)}, u32[]{:S(2)}) copy-start(bf16[6,3,2,256,128]{4,3,2,1,0:T(8,128)(2,1)} %param.4) | copy-start | bytes 7077892
  7.2 31.4 %collective-permute-start.1 = (bf16[6,3,2,256,128]{4,3,2,1,0:T(8,128)(2,1)}, bf16[6,3,2,256,128]{4,3,2,1,0:T(8,128)(2,1)S(1)}, u32[]{:S(2)}, u32[]{:S(2)}) collective-permute-start(bf16[6,3,2,256,128]{4,3,2,1,0:T(8,128)(2,1)} %param.4), channel_id=1, source_target_pairs={{1,0},{2,1},{3,2},{4,3},{5,4},{6,5},{7,6},{8,7},{9,8},{10,9},{11,1... | collective-permute-start | bytes 7077896 | tf_op jit(solution)/shard_map/ppermute | solution.py:18
  10.6 53.6 %collective-permute-start = (bf16[6,3,2,256,128]{4,3,2,1,0:T(8,128)(2,1)}, bf16[6,3,2,256,128]{4,3,2,1,0:T(8,128)(2,1)S(1)}, u32[]{:S(2)}, u32[]{:S(2)}) collective-permute-start(bf16[6,3,2,256,128]{4,3,2,1,0:T(8,128)(2,1)} %param.4), channel_id=1, source_target_pairs={{0,1},{1,2},{2,3},{3,4},{4,5},{5,6},{6,7},{7,8},{8,9},{9,10},{10,1... | collective-permute-start | bytes 7077896 | tf_op jit(solution)/shard_map/ppermute | solution.py:15
  206.9 173.2 %all-to-all-start.1 = ((bf16[48,12,2,32,128]{4,2,1,0,3:T(2,128)(2,1)}), bf16[48,12,2,32,128]{4,2,1,0,3:T(2,128)(2,1)}, u32[]{:S(2)}, u32[]{:S(2)}) async-start(bf16[48,12,2,32,128]{4,2,1,0,3:T(2,128)(2,1)} %copy.57), calls=%async_computation.1 | async-start | bytes 18874368 | tf_op jit(solution)/shard_map/all_to_all | solution.py:40
  236.5 832.2 %all-reduce.4.cloned.1.call-start = ((), (), s32[]{:S(2)}) async-start(), calls=%async_computation.2 | async-start | bytes 2359296
Sparse Core Ops, SparseCore 0:
  923.2 145.5 all-reduce.3
where the time goes:
time: 1080 us
  waiting for transfers between devices  335 us (31%)
  local copies, waits for them, and re-layouts  262 us (24%)
  other arithmetic  193 us (18%)
  blocking collectives  140 us (13%)
  matrix products  95.9 us (9%)
  starting transfers between devices  36.5 us (3%)
  between operations  14.1 us (1%)
    convert_element_type x8, other arithmetic, one_step(): carried = (carried * piece_weights).astype(jnp.bfloat16).reshape(mode_cou...  159 us
    unnamed x2, waiting for transfers between devices  145 us
    all_to_all x1, waiting for transfers between devices, regroup(): lax.all_to_all(lax.all_to_all(stacked, 'mode', split_axis=3, concat_axis=...  143 us
    while x32, local copies, waits for them, and re-layouts  90.8 us
    dot_general x8, matrix products, one_step(): lax.dot_general(piece_values.reshape(mode_count, 3 * block_size), carried...  81 us
    psum x1, blocking collectives, per_device(): diss_sum = lax.psum(diss_part, ('mode', 'slab'))  70.5 us
    all_to_all x1, blocking collectives, regroup(): lax.all_to_all(stacked, 'mode', split_axis=3, concat_axis=0, tiled=True)  69.1 us
    all_to_all x3, local copies, waits for them, and re-layouts, regroup(): lax.all_to_all(stacked, 'mode', split_axis=3, concat_axis=0, tiled=True)  35.1 us
  transfers between devices with their start and end apart: 4, of which 4 were waited for; matrix products, arithmetic and copies ran while one was open for 0% of the time, Pallas kernels for 0%

commit v1 on v0

--- a/solution.py
+++ b/solution.py
@@ -107,7 +107,7 @@
     grad_all = regrouped[:, 3:].reshape((regrouped.shape[0], 3, 3) + regrouped.shape[2:])
     conv_part, diss_part = contract(values, grad_all, volume, 1024)
     conv_sum = lax.psum_scatter(conv_part, ("mode", "slab"), scatter_dimension=0, tiled=True)
-    diss_sum = lax.psum(diss_part, ("mode", "slab"))
+    diss_sum = jnp.sum(lax.all_gather(diss_part, ("mode", "slab")), axis=0)
     cell_total = (
         volume.shape[0]
         * volume.shape[1]

time: 1080 us -> 1210 us (1.12)
  waiting for transfers between devices: 335 us -> 539 us
  blocking collectives: 140 us -> 69.1 us
    all_gather x0 -> x1, waiting for transfers between devices: none -> 196 us  [per_device(): diss_sum = jnp.sum(lax.all_gather(diss_part, ('mode', 'slab')), axis=0)]
    psum x1 -> x0, blocking collectives: 70.5 us -> none  [per_device(): diss_sum = lax.psum(diss_part, ('mode', 'slab'))]
    unnamed x2 -> x3, waiting for transfers between devices: 145 us -> 153 us
  transfers between devices with their start and end apart: 4 -> 5, of which waited for: 4 -> 5; matrix products, arithmetic and copies ran while one was open for 0% -> 0% of each run, Pallas kernels for 0% -> 0%
where the time goes in v1:
time: 1210 us
  waiting for transfers between devices  539 us (45%)
  local copies, waits for them, and re-layouts  261 us (22%)
  other arithmetic  195 us (16%)
  matrix products  95.8 us (8%)
  blocking collectives  69.1 us (6%)
  starting transfers between devices  36.5 us (3%)
  between operations  14.1 us (1%)
    all_gather x1, waiting for transfers between devices, per_device(): diss_sum = jnp.sum(lax.all_gather(diss_part, ('mode', 'slab')), axis=0)  196 us
    convert_element_type x8, other arithmetic, one_step(): carried = (carried * piece_weights).astype(jnp.bfloat16).reshape(mode_cou...  159 us
    unnamed x3, waiting for transfers between devices  153 us
    all_to_all x1, waiting for transfers between devices, regroup(): lax.all_to_all(lax.all_to_all(stacked, 'mode', split_axis=3, concat_axis=...  143 us
    while x32, local copies, waits for them, and re-layouts  89.9 us
    dot_general x8, matrix products, one_step(): lax.dot_general(piece_values.reshape(mode_count, 3 * block_size), carried...  80.9 us
    all_to_all x1, blocking collectives, regroup(): lax.all_to_all(stacked, 'mode', split_axis=3, concat_axis=0, tiled=True)  69.1 us
    all_to_all x3, local copies, waits for them, and re-layouts, regroup(): lax.all_to_all(stacked, 'mode', split_axis=3, concat_axis=0, tiled=True)  35.1 us
  transfers between devices with their start and end apart: 5, of which 5 were waited for; matrix products, arithmetic and copies ran while one was open for 0% of the time, Pallas kernels for 0%

profile of v1, /device:TPU:1, one launch (start us, length us, event | category | flops | bytes accessed | tf_op | source)
XLA Modules:
  0.0 1211.6 jit_solution(5641633230011245620)
XLA Ops:
  17.1 21.5 %collective-permute-done.1 = bf16[6,3,2,256,128]{4,3,2,1,0:T(8,128)(2,1)S(1)} collective-permute-done((bf16[6,3,2,256,128]{4,3,2,1,0:T(8,128)(2,1)}, bf16[6,3,2,256,128]{4,3,2,1,0:T(8,128)(2,1)S(1)}, u32[]{:S(2)}, u32[]{:S(2)}) %collective-permute-start.1) | collective-permute-done | bytes 2359328 | tf_op jit(solution)/shard_map/ppermute | solution.py:18
  38.6 25.6 %collective-permute-done = bf16[6,3,2,256,128]{4,3,2,1,0:T(8,128)(2,1)S(1)} collective-permute-done((bf16[6,3,2,256,128]{4,3,2,1,0:T(8,128)(2,1)}, bf16[6,3,2,256,128]{4,3,2,1,0:T(8,128)(2,1)S(1)}, u32[]{:S(2)}, u32[]{:S(2)}) %collective-permute-start) | collective-permute-done | bytes 2359328 | tf_op jit(solution)/shard_map/ppermute | solution.py:15
  85.1 17.6 %copy.54 = bf16[6,12,2,256,128]{4,2,1,0,3:T(2,128)(2,1)S(1)} copy(bf16[6,12,2,256,128]{4,3,2,1,0:T(8,128)(2,1)} %pad_maximum_fusion) | data formatting | bytes 18874368 | tf_op jit(solution)/shard_map/concatenate | solution.py:102
  102.7 69.1 %all_to_all.36 = bf16[6,12,2,256,128]{4,2,1,0,3:T(2,128)(2,1)} all-to-all(bf16[6,12,2,256,128]{4,2,1,0,3:T(2,128)(2,1)S(1)} %copy.54), channel_id=1, replica_groups=mesh['mode'=8,'slab'=16] {'mode'}, dimensions={3} | all-to-all | bytes 18874368 | tf_op jit(solution)/shard_map/all_to_all | solution.py:41
  181.7 10.4 copy.56
  192.1 14.8 %copy.57 = bf16[48,12,2,32,128]{4,2,1,0,3:T(2,128)(2,1)} copy(bf16[48,12,2,32,128]{4,3,2,1,0:T(8,128)(2,1)} %bitcast.75) | data formatting | bytes 18874368 | tf_op jit(solution)/shard_map/all_to_all | solution.py:41
  206.9 29.6 %all-to-all-start.1 = ((bf16[48,12,2,32,128]{4,2,1,0,3:T(2,128)(2,1)}), bf16[48,12,2,32,128]{4,2,1,0,3:T(2,128)(2,1)}, u32[]{:S(2)}, u32[]{:S(2)}) async-start(bf16[48,12,2,32,128]{4,2,1,0,3:T(2,128)(2,1)} %copy.57), calls=%async_computation.1 | async-start | bytes 18874368 | tf_op jit(solution)/shard_map/all_to_all | solution.py:40
  236.8 143.2 %all-to-all-done.1 = bf16[48,12,2,32,128]{4,2,1,0,3:T(2,128)(2,1)} async-done(((bf16[48,12,2,32,128]{4,2,1,0,3:T(2,128)(2,1)}), bf16[48,12,2,32,128]{4,2,1,0,3:T(2,128)(2,1)}, u32[]{:S(2)}, u32[]{:S(2)}) %all-to-all-start.1) | async-done | bytes 9437216 | tf_op jit(solution)/shard_map/all_to_all | solution.py:40
  389.4 10.3 copy.59
  415.6 16.2 %reshape_reshape.3 = bf16[48,3,3,8192]{3,0,2,1:T(8,128)(2,1)} reshape(bf16[48,9,32,2,128]{4,3,2,0,1:T(2,128)(2,1)} %copy.61) | data formatting | bytes 14155776 | tf_op jit(solution)/shard_map/reshape;reshape | solution.py:54
  441.9 406.8 %while.16 = (s32[]{:T(128)}, f32[48,2304]{1,0:T(8,128)}, f32[48,48]{1,0:T(8,128)S(1)}, bf16[48,3,8192]{2,1,0:T(4,128)(2,1)}, bf16[48,3,3,8192]{3,0,2,1:T(8,128)(...) while((s32[]{:T(128)}, f32[48,2304]{1,0:T(8,128)}, ...), condition=%wide.region_1.2_spmd.clone, body=%wide.region_0.1_spmd.clone.sunk | while | flops 773485056 | bytes 75239088 | solution.py:91
  452.6 19.9 %multiply_convert_fusion.9 = bf16[48,48,3,1024]{3,2,1,0:T(4,128)(2,1)S(1)} fusion(f32[1024]{0:T(1024)S(1)} %dynamic_slice.40, f32[48,3,1024]{2,1,0:T(4,128)} %copy.84, f32[48,1024]{1,0:T(8,128)} %get-tuple-element.238, f32[48,3,1024]{2,1,0:T(4,128)} %copy.85, f32[48,1024]{1,0:T(8,128)} %get-tuple-element.240, f32[48,3,1024]{2,1,0:T(4,128)} %copy.86, ...), kind=kLoop, calls=%fused_computation.clone.1 | loop fusion | flops 49545216 | bytes 16519168 | tf_op jit(solution)/shard_map/while/body/eval_jaxpr/convert_element_type | solution.py:69
  472.5 10.3 copy.88
  503.4 19.9 %multiply_convert_fusion.9 = bf16[48,48,3,1024]{3,2,1,0:T(4,128)(2,1)S(1)} fusion(f32[1024]{0:T(1024)S(1)} %dynamic_slice.40, f32[48,3,1024]{2,1,0:T(4,128)} %copy.84, f32[48,1024]{1,0:T(8,128)} %get-tuple-element.238, f32[48,3,1024]{2,1,0:T(4,128)} %copy.85, f32[48,1024]{1,0:T(8,128)} %get-tuple-element.240, f32[48,3,1024]{2,1,0:T(4,128)} %copy.86, ...), kind=kLoop, calls=%fused_computation.clone.1 | loop fusion | flops 49545216 | bytes 16519168 | tf_op jit(solution)/shard_map/while/body/eval_jaxpr/convert_element_type | solution.py:69
  523.3 10.3 copy.88
  554.2 19.9 %multiply_convert_fusion.9 = bf16[48,48,3,1024]{3,2,1,0:T(4,128)(2,1)S(1)} fusion(f32[1024]{0:T(1024)S(1)} %dynamic_slice.40, f32[48,3,1024]{2,1,0:T(4,128)} %copy.84, f32[48,1024]{1,0:T(8,128)} %get-tuple-element.238, f32[48,3,1024]{2,1,0:T(4,128)} %copy.85, f32[48,1024]{1,0:T(8,128)} %get-tuple-element.240, f32[48,3,1024]{2,1,0:T(4,128)} %copy.86, ...), kind=kLoop, calls=%fused_computation.clone.1 | loop fusion | flops 49545216 | bytes 16519168 | tf_op jit(solution)/shard_map/while/body/eval_jaxpr/convert_element_type | solution.py:69
  574.1 10.3 copy.88
  584.4 10.1 convolution_add_fusion.2
  605.1 19.9 %multiply_convert_fusion.9 = bf16[48,48,3,1024]{3,2,1,0:T(4,128)(2,1)S(1)} fusion(f32[1024]{0:T(1024)S(1)} %dynamic_slice.40, f32[48,3,1024]{2,1,0:T(4,128)} %copy.84, f32[48,1024]{1,0:T(8,128)} %get-tuple-element.238, f32[48,3,1024]{2,1,0:T(4,128)} %copy.85, f32[48,1024]{1,0:T(8,128)} %get-tuple-element.240, f32[48,3,1024]{2,1,0:T(4,128)} %copy.86, ...), kind=kLoop, calls=%fused_computation.clone.1 | loop fusion | flops 49545216 | bytes 16519168 | tf_op jit(solution)/shard_map/while/body/eval_jaxpr/convert_element_type | solution.py:69
  625.0 10.3 copy.88
  635.2 10.1 convolution_add_fusion.2
  655.9 19.9 %multiply_convert_fusion.9 = bf16[48,48,3,1024]{3,2,1,0:T(4,128)(2,1)S(1)} fusion(f32[1024]{0:T(1024)S(1)} %dynamic_slice.40, f32[48,3,1024]{2,1,0:T(4,128)} %copy.84, f32[48,1024]{1,0:T(8,128)} %get-tuple-element.238, f32[48,3,1024]{2,1,0:T(4,128)} %copy.85, f32[48,1024]{1,0:T(8,128)} %get-tuple-element.240, f32[48,3,1024]{2,1,0:T(4,128)} %copy.86, ...), kind=kLoop, calls=%fused_computation.clone.1 | loop fusion | flops 49545216 | bytes 16519168 | tf_op jit(solution)/shard_map/while/body/eval_jaxpr/convert_element_type | solution.py:69
  675.8 10.3 copy.88
  706.8 19.9 %multiply_convert_fusion.9 = bf16[48,48,3,1024]{3,2,1,0:T(4,128)(2,1)S(1)} fusion(f32[1024]{0:T(1024)S(1)} %dynamic_slice.40, f32[48,3,1024]{2,1,0:T(4,128)} %copy.84, f32[48,1024]{1,0:T(8,128)} %get-tuple-element.238, f32[48,3,1024]{2,1,0:T(4,128)} %copy.85, f32[48,1024]{1,0:T(8,128)} %get-tuple-element.240, f32[48,3,1024]{2,1,0:T(4,128)} %copy.86, ...), kind=kLoop, calls=%fused_computation.clone.1 | loop fusion | flops 49545216 | bytes 16519168 | tf_op jit(solution)/shard_map/while/body/eval_jaxpr/convert_element_type | solution.py:69
  726.7 10.3 copy.88
  757.6 19.9 %multiply_convert_fusion.9 = bf16[48,48,3,1024]{3,2,1,0:T(4,128)(2,1)S(1)} fusion(f32[1024]{0:T(1024)S(1)} %dynamic_slice.40, f32[48,3,1024]{2,1,0:T(4,128)} %copy.84, f32[48,1024]{1,0:T(8,128)} %get-tuple-element.238, f32[48,3,1024]{2,1,0:T(4,128)} %copy.85, f32[48,1024]{1,0:T(8,128)} %get-tuple-element.240, f32[48,3,1024]{2,1,0:T(4,128)} %copy.86, ...), kind=kLoop, calls=%fused_computation.clone.1 | loop fusion | flops 49545216 | bytes 16519168 | tf_op jit(solution)/shard_map/while/body/eval_jaxpr/convert_element_type | solution.py:69
  777.5 10.3 copy.88
  787.8 10.1 convolution_add_fusion.2
  808.4 19.9 %multiply_convert_fusion.9 = bf16[48,48,3,1024]{3,2,1,0:T(4,128)(2,1)S(1)} fusion(f32[1024]{0:T(1024)S(1)} %dynamic_slice.40, f32[48,3,1024]{2,1,0:T(4,128)} %copy.84, f32[48,1024]{1,0:T(8,128)} %get-tuple-element.238, f32[48,3,1024]{2,1,0:T(4,128)} %copy.85, f32[48,1024]{1,0:T(8,128)} %get-tuple-element.240, f32[48,3,1024]{2,1,0:T(4,128)} %copy.86, ...), kind=kLoop, calls=%fused_computation.clone.1 | loop fusion | flops 49545216 | bytes 16519168 | tf_op jit(solution)/shard_map/while/body/eval_jaxpr/convert_element_type | solution.py:69
  828.3 10.3 copy.88
  852.3 152.4 %all-reduce.4.cloned.1.call-done = f32[2304,48]{1,0:T(8,128)} async-done(((f32[2304,48]{1,0:T(8,128)}), f32[2304,48]{1,0:T(8,128)}) %all-reduce.4.cloned.1.call-update) | async-done | bytes 442384
  1006.1 195.9 %all-gather.3.cloned.1.call-done = f32[6144,48]{1,0:T(8,128)} async-done(((f32[48,48]{1,0:T(8,128)}), f32[6144,48]{1,0:T(8,128)}) %all-gather.3.cloned.1.call-update) | async-done | bytes 1179664 | tf_op jit(solution)/shard_map/all_gather | solution.py:110
  (128 shorter events, 218.8 us)
Async XLA Ops:
  7.2 57.0 %copy-start = (bf16[6,3,2,256,128]{4,3,2,1,0:T(8,128)(2,1)S(1)}, bf16[6,3,2,256,128]{4,3,2,1,0:T(8,128)(2,1)}, u32[]{:S(2)}) copy-start(bf16[6,3,2,256,128]{4,3,2,1,0:T(8,128)(2,1)} %param.4) | copy-start | bytes 7077892
  7.2 31.4 %collective-permute-start.1 = (bf16[6,3,2,256,128]{4,3,2,1,0:T(8,128)(2,1)}, bf16[6,3,2,256,128]{4,3,2,1,0:T(8,128)(2,1)S(1)}, u32[]{:S(2)}, u32[]{:S(2)}) collective-permute-start(bf16[6,3,2,256,128]{4,3,2,1,0:T(8,128)(2,1)} %param.4), channel_id=1, source_target_pairs={{1,0},{2,1},{3,2},{4,3},{5,4},{6,5},{7,6},{8,7},{9,8},{10,9},{11,1... | collective-permute-start | bytes 7077896 | tf_op jit(solution)/shard_map/ppermute | solution.py:18
  10.6 53.6 %collective-permute-start = (bf16[6,3,2,256,128]{4,3,2,1,0:T(8,128)(2,1)}, bf16[6,3,2,256,128]{4,3,2,1,0:T(8,128)(2,1)S(1)}, u32[]{:S(2)}, u32[]{:S(2)}) collective-permute-start(bf16[6,3,2,256,128]{4,3,2,1,0:T(8,128)(2,1)} %param.4), channel_id=1, source_target_pairs={{0,1},{1,2},{2,3},{3,4},{4,5},{5,6},{6,7},{7,8},{8,9},{9,10},{10,1... | collective-permute-start | bytes 7077896 | tf_op jit(solution)/shard_map/ppermute | solution.py:15
  206.9 173.1 %all-to-all-start.1 = ((bf16[48,12,2,32,128]{4,2,1,0,3:T(2,128)(2,1)}), bf16[48,12,2,32,128]{4,2,1,0,3:T(2,128)(2,1)}, u32[]{:S(2)}, u32[]{:S(2)}) async-start(bf16[48,12,2,32,128]{4,2,1,0,3:T(2,128)(2,1)} %copy.57), calls=%async_computation.1 | async-start | bytes 18874368 | tf_op jit(solution)/shard_map/all_to_all | solution.py:40
  236.5 768.2 %all-reduce.4.cloned.1.call-start = ((), (), s32[]{:S(2)}) async-start(), calls=%async_computation.3 | async-start | bytes 2359296
  848.7 2.9 copy-start.1
  851.5 350.4 %all-gather.3.cloned.1.call-start = ((), (), s32[]{:S(2)}) async-start(), calls=%async_computation.2 | async-start | bytes 3170304 | tf_op jit(solution)/shard_map/all_gather | solution.py:110
Sparse Core Ops, SparseCore 0:
  851.7 153.0 all-reduce.3
  1007.0 194.8 all-gather.2
